TPU v7x, 32 devices: a whole 2x2x4 slice. The times are simulated.
32 devices in a mesh: perm: 2 (over y), subj: 8 (over z, core), vert: 2 (over x).
Axes of the slice: x: 2, y: 2, z: 4, core: 2. Of those that a mesh axis runs over, the one named last changes fastest.
Arguments:
- kinship: bfloat16 [2048, 2048], P('subj')
- phenotype: bfloat16 [2048, 2048], P('subj', 'vert')
- shuffle: int32 [4096], P(('perm', 'subj')), parts along dimension 0, may hold values from 0 to 2047, as said below
Outputs:
- statistic: float32 [4096], P(('perm', 'vert')), parts along dimension 0
There are 2 independent parts, one for each index of `perm`. A program takes and returns all parts, laid end to end along the dimension named above; an argument that names none is the same for every part. Nothing has to cross between parts.
Inputs may be any that keep to these rules, and one draw needn't show every extreme that they name: shuffle is a permutation of 0 to 2047 that maps every subject into its own exchangeability block.
All inputs are finite; a program needn't handle non-finite values.
Results may differ from a plain program's by a relative error of at most 0.0003.
Values may be sent and summed in bfloat16 or wider, within the bound.
A program may use at most 128 MiB of HBM per device.

v0:
```python
import jax
import jax.numpy as jnp
from jax import lax
from jax.sharding import PartitionSpec as P


def per_device(kinship, phenotype, shuffle):
    row_count = phenotype.shape[0]
    subject_count = kinship.shape[1]
    row_offset = lax.axis_index("subj") * row_count
    shuffle_all = lax.all_gather(shuffle, "subj", axis=0, tiled=True)
    own_block = lax.dynamic_slice_in_dim(kinship, row_offset, row_count, 1)
    kin_diag = jnp.diagonal(own_block).astype(jnp.float32)
    inverse = (
        jnp.zeros((subject_count,), jnp.int32)
        .at[shuffle_all]
        .set(jnp.arange(subject_count, dtype=jnp.int32))
    )
    kin_moved = jnp.take(kinship, inverse, axis=1)
    piece = lax.all_gather(phenotype, "subj", axis=0, tiled=True)
    piece_rows = piece.shape[0]
    targets = jnp.arange(piece_rows, dtype=jnp.int32)
    picker = (shuffle[:, None] == targets[None, :]).astype(jnp.bfloat16)
    product = jnp.dot(kin_moved, piece, preferred_element_type=jnp.float32)
    picked = jnp.dot(picker, piece, preferred_element_type=jnp.float32)
    local_perm = picked.astype(jnp.bfloat16)
    moved = local_perm.astype(jnp.float32)
    cross_term = jnp.sum(moved * (product - kin_diag[:, None] * moved), axis=0)
    values = phenotype.astype(jnp.float32)
    squares = jnp.sum(values * values, axis=0)
    cross_all, squares_all = lax.psum((cross_term, squares), "subj")
    return cross_all / (
        jnp.sqrt(jnp.float32(subject_count)) * (squares_all / subject_count + 1e-05)
    )


def solution(mesh):
    in_specs = (P("subj", None), P("subj", "vert"), P(("perm", "subj")))
    out_specs = P(("perm", "vert"))
    return jax.shard_map(
        per_device, mesh=mesh, in_specs=in_specs, out_specs=out_specs, check_vma=False
    )
```

profile of v0, /device:TPU:0, one launch (start us, length us, event | category | flops | bytes accessed | tf_op | source)
XLA Modules:
  0.0 86.2 jit_solution(4435707539312031258)
XLA Ops:
  6.5 0.0 all-gather.3.cloned.1.call-start
  6.5 0.7 all-gather.3.cloned.1.call-update
  7.3 1.5 %copy.6 = bf16[256,2048]{0,1:T(8,128)(2,1)S(1)} copy(bf16[256,2048]{1,0:T(8,128)(2,1)} %param.3) | data formatting | bytes 2097152 | tf_op args[0]
  8.8 0.9 %constant_dynamic-slice_fusion = bf16[256,256]{1,0:T(8,128)(2,1)S(1)} fusion(bf16[256,2048]{1,0:T(8,128)(2,1)} %param.3, s32[]{:T(128)S(6)} %select_n.22), kind=kLoop, calls=%fused_computation.23 | loop fusion | bytes 262148 | tf_op jit(solution)/shard_map/dynamic_slice | solution.py:12
  9.7 2.5 %gather_fusion.1 = bf16[256]{0:T(256)(128)(2,1)S(1)} fusion(bf16[256,256]{1,0:T(8,128)(2,1)S(1)} %constant_dynamic-slice_fusion, s32[256]{0:T(256)S(1)} %bitcast.5), kind=kCustom, calls=%fused_computation.1 | custom fusion | bytes 3072 | tf_op jit(solution)/shard_map/jit(diagonal)/cond/branch_0_fun/gather | solution.py:13
  12.2 13.7 %all-gather = s32[8,1,256]{2,1,0:T(1,128)S(1)} all-gather(s32[1,1,256]{2,1,0:T(1,128)} %bitcast.7), channel_id=1, replica_groups=mesh['perm'=2,'subj'=8,'vert'=2] {'subj'}, dimensions={0}, use_global_device_ids=true | all-gather | bytes 9216 | tf_op jit(solution)/shard_map/all_gather | solution.py:11
  26.0 8.0 %scatter_custom_fusion = s32[2048]{0:T(1024)S(1)} fusion(s32[2048]{0:T(1024)S(1)} %compare_select_fusion.1, s32[2048]{0:T(1024)S(1)} %iota.16, s32[]{:T(128)} %constant.12.clone.1), kind=kCustom, calls=%fused_computation.20 | custom fusion | bytes 8196 | tf_op jit(solution)/shard_map/scatter | solution.py:17
  34.0 0.0 copy-start
  34.0 0.0 copy-start.1
  34.0 7.5 %gather_fusion = bf16[2048,256]{1,0:T(8,128)(2,1)S(1)} fusion(bf16[256,2048]{0,1:T(8,128)(2,1)S(1)} %copy.6, s32[2048]{0:T(1024)S(1)} %fusion.7), kind=kCustom, calls=%fused_computation | custom fusion | bytes 2105344 | tf_op jit(solution)/shard_map/jit(_take)/gather | solution.py:19
  41.5 0.0 copy-done
  41.6 0.1 multiply_reduce_fusion
  41.7 16.9 %all-gather.3.cloned.1.call-done = bf16[2048,1024]{1,0:T(8,128)(2,1)} async-done(((bf16[256,1024]{1,0:T(8,128)(2,1)}), bf16[2048,1024]{1,0:T(8,128)(2,1)}) %all-gather.3.cloned.1.call-update) | async-done | bytes 4194320 | tf_op jit(solution)/shard_map/all_gather | solution.py:20
  58.6 0.0 copy-done.1
  58.6 0.0 copy-start.2
  58.6 3.6 %fusion.1 = bf16[256,1024]{1,0:T(8,128)(2,1)S(1)} fusion(bf16[2048,1024]{1,0:T(8,128)(2,1)} %all-gather.3.cloned.1.call-done, s32[256]{0:T(256)S(1)} %copy-done.1), kind=kOutput, calls=%fused_computation.8 | convolution fusion | flops 1074528256 | bytes 4719616 | tf_op jit(solution)/shard_map/dot_general | solution.py:25
  62.2 0.0 copy-done.2
  62.2 1.5 %fusion.2 = f32[1024]{0:T(1024)S(1)} fusion(bf16[2048,1024]{1,0:T(8,128)(2,1)S(1)} %copy-done.2, bf16[256,1024]{1,0:T(8,128)(2,1)S(1)} %fusion.1, bf16[2048,256]{1,0:T(8,128)(2,1)S(1)} %gather_fusion, pred[2048]{0:T(1024)(128)(4,1)S(1)} %compare_and_fusion, f32[256]{0:T(256)S(1)} %convert_element_type.19), kind=kOutput, calls=%fused_computation.9 | convolution fusion | flops 1075575808 | bytes 5774336 | tf_op jit(solution)/shard_map/dot_general | solution.py:24
  63.7 15.1 %all-reduce = (f32[1024]{0:T(1024)S(1)}, f32[1024]{0:T(1024)S(1)}) all-reduce(f32[1024]{0:T(1024)S(1)} %fusion.2, f32[1024]{0:T(1024)S(1)} %multiply_reduce_fusion), channel_id=1, replica_groups=mesh['perm'=2,'subj'=8,'vert'=2] {'subj'}, use_global_device_ids=true, to_apply=%region_2.3 | all-reduce | flops 2048 | bytes 16384 | tf_op jit(solution)/shard_map/psum | solution.py:31
  78.8 0.6 multiply_divide_fusion
  (6 shorter events, 0.0 us)
Async XLA Ops:
  6.5 52.0 %all-gather.3.cloned.1.call-start = ((), (), s32[]{:S(2)}) async-start(), calls=%async_computation | async-start | bytes 4718592 | tf_op jit(solution)/shard_map/all_gather | solution.py:20
  34.0 7.5 %copy-start = (bf16[256,1024]{1,0:T(8,128)(2,1)S(1)}, bf16[256,1024]{1,0:T(8,128)(2,1)}, u32[]{:S(2)}) copy-start(bf16[256,1024]{1,0:T(8,128)(2,1)} %param.4) | copy-start | bytes 1572868
  34.0 24.5 %copy-start.1 = (s32[256]{0:T(256)S(1)}, s32[256]{0:T(256)}, u32[]{:S(2)}) copy-start(s32[256]{0:T(256)} %param.5) | copy-start | bytes 3076
  58.6 3.6 %copy-start.2 = (bf16[2048,1024]{1,0:T(8,128)(2,1)S(1)}, bf16[2048,1024]{1,0:T(8,128)(2,1)}, u32[]{:S(2)}) copy-start(bf16[2048,1024]{1,0:T(8,128)(2,1)} %all-gather.3.cloned.1.call-done) | copy-start | bytes 12582916
Sparse Core Ops, SparseCore 0:
  8.9 49.5 all-gather.2
where the time goes:
time: 86.4 us; the launch traced here: 86.2 us
  blocking collectives  28.8 us (33%)
  local copies, waits for them, and re-layouts  20.5 us (24%)
  waiting for transfers between devices  17.6 us (20%)
  between operations  13.5 us (16%)
  matrix products  5.08 us (6%)
    all_gather x1, waiting for transfers between devices, per_device(): piece = lax.all_gather(phenotype, 'subj', axis=0, tiled=True)  16.9 us
    psum x1, blocking collectives, per_device(): cross_all, squares_all = lax.psum((cross_term, squares), 'subj')  15.1 us
    all_gather x1, blocking collectives, per_device(): shuffle_all = lax.all_gather(shuffle, 'subj', axis=0, tiled=True)  13.7 us
    scatter x1, local copies, waits for them, and re-layouts, per_device(): inverse = jnp.zeros((subject_count,), jnp.int32).at[shuffle_all].set(jnp....  8.05 us
    gather x1, local copies, waits for them, and re-layouts, per_device(): kin_moved = jnp.take(kinship, inverse, axis=1)  7.5 us
    dot_general x1, matrix products, per_device(): picked = jnp.dot(picker, piece, preferred_element_type=jnp.float32)  3.62 us
    gather x1, local copies, waits for them, and re-layouts, per_device(): kin_diag = jnp.diagonal(own_block).astype(jnp.float32)  2.49 us
  transfers between devices with their start and end apart: 1, of which 1 were waited for; matrix products, arithmetic and copies ran while one was open for 24% of the time, Pallas kernels for 0%

commit v1 on v0

v1 whole, which is shorter than its diff:
```python
import functools

import jax
import jax.numpy as jnp
from jax import lax
from jax.experimental import pallas as pl
from jax.experimental.pallas import tpu as pltpu
from jax.sharding import PartitionSpec as P

MESH = pl.DeviceIdType.MESH
CORES = 2
HALVES = 2


def kernel(
    n_perm, n_subj,
    kin_ref, phe_ref, shf_ref, out_ref,
    shuf, scol, moved_kin, gathered, acc, parts, final,
    shuf_send, shuf_recv, own_send, row_send, sib_send, row_recv, fin_send, fin_recv,
):
    perm, subj = lax.axis_index("perm"), lax.axis_index("subj")
    n_all = n_perm * n_subj
    me = perm * n_subj + subj
    z, core = subj // CORES, subj % CORES
    n_z = n_subj // CORES
    sibling = z * CORES + (1 - core)
    rows = kin_ref.shape[0]
    cols = gathered.shape[2]
    piece = rows // HALVES
    first_col = pl.multiple_of(perm * cols, cols)
    n_events = HALVES * (n_z - 1)

    def partner(k):
        other = lax.rem(me + k, n_all)
        return other, {"perm": other // n_subj, "subj": lax.rem(other, n_subj)}

    barrier = pltpu.get_barrier_semaphore()

    @pl.loop(1, n_all)
    def _(k):
        pl.semaphore_signal(barrier, inc=1, device_id=partner(k)[1], device_id_type=MESH)

    pl.semaphore_wait(barrier, n_all - 1)

    def half(h):
        return pl.ds(pl.multiple_of(h * piece, piece), piece)

    def own_copy(h, way, target):
        return pltpu.make_async_remote_copy(
            src_ref=phe_ref.at[half(h), pl.ds(first_col, cols)],
            dst_ref=gathered.at[subj, half(h)],
            send_sem=own_send.at[way, h], recv_sem=row_recv.at[subj, h],
            device_id={"subj": target}, device_id_type=MESH)

    def pass_copy(slot, h, sems, target):
        return pltpu.make_async_remote_copy(
            src_ref=gathered.at[slot, half(h)], dst_ref=gathered.at[slot, half(h)],
            send_sem=sems.at[slot, h], recv_sem=row_recv.at[slot, h],
            device_id={"subj": target}, device_id_type=MESH)

    def shuf_copy(k, slot):
        return pltpu.make_async_remote_copy(
            src_ref=shf_ref, dst_ref=shuf.at[slot],
            send_sem=shuf_send.at[k], recv_sem=shuf_recv.at[slot],
            device_id=partner(k)[1], device_id_type=MESH)

    @pl.loop(1, n_all)
    def _(k):
        shuf_copy(k, me).start()

    def own_sends(act):
        for h in range(HALVES):
            @pl.when(z > 0)
            def _():
                act(own_copy(h, 0, subj - CORES))

            @pl.when(z < n_z - 1)
            def _():
                act(own_copy(h, 1, subj + CORES))

            act(own_copy(h, 2, sibling))

    own_sends(lambda copy: copy.start())
    shuf[me] = shf_ref[...]
    own = phe_ref[:, pl.ds(first_col, cols)]
    gathered[subj] = own
    own32 = own.astype(jnp.float32)
    squares = jnp.sum(own32 * own32, axis=0, keepdims=True)
    for p in range(n_perm):
        parts[p, 1:2] = squares
    own_cols = pl.ds(pl.multiple_of(subj * rows, rows), rows)
    down = lax.broadcasted_iota(jnp.int32, (rows, rows), 0)
    across = lax.broadcasted_iota(jnp.int32, (rows, rows), 1)
    kin_diag = jnp.sum(
        jnp.where(down == across, kin_ref[:, own_cols].astype(jnp.float32), 0.0),
        axis=1, keepdims=True)

    @pl.loop(1, n_all)
    def _(k):
        shuf_copy(k, partner(k)[0]).wait_recv()

    for p in range(n_perm):
        mine = shuf[p * n_subj + subj]
        scol[p] = jnp.transpose(jnp.broadcast_to(mine, (rows, rows)))

    def move(task):
        p, block = task // n_subj, lax.rem(task, n_subj)
        base = down + block * rows
        picks = jnp.concatenate(
            [(base == shuf[p * n_subj + j]).astype(jnp.bfloat16) for j in range(n_subj)],
            axis=1)
        kin = lax.dot_general(
            kin_ref[...], picks, (((1,), (1,)), ((), ())),
            preferred_element_type=jnp.float32)
        at = pl.multiple_of(p * 2 * rows, 2 * rows)
        moved_kin[block, pl.ds(at, rows)] = kin.astype(jnp.bfloat16)
        picker = (scol[p] == across + block * rows).astype(jnp.bfloat16)
        moved_kin[block, pl.ds(at + rows, rows)] = picker

    def event(e, act):
        dist, h = e // HALVES + 1, lax.rem(e, HALVES)

        @pl.when(z + dist < n_z)
        def _():
            act(subj + CORES * dist, h, z > 0, subj - CORES)

        @pl.when(z - dist >= 0)
        def _():
            act(subj - CORES * dist, h, z < n_z - 1, subj + CORES)

    def arrive(slot, h, onward, target):
        pass_copy(slot, h, row_send, sibling).wait_recv()

        @pl.when(onward)
        def _():
            pass_copy(slot, h, row_send, target).start()

        pass_copy(slot, h, sib_send, sibling).start()

    def drain(slot, h, onward, target):
        @pl.when(onward)
        def _():
            pass_copy(slot, h, row_send, target).wait_send()

        pass_copy(slot, h, sib_send, sibling).wait_send()

    def add(slot):
        acc[...] += jnp.dot(
            moved_kin[slot], gathered[slot], preferred_element_type=jnp.float32)

    def await_sibling(slot):
        for h in range(HALVES):
            pass_copy(slot, h, row_send, sibling).wait_recv()

    def add_dist(dist):
        def pair(slot, other):
            add(slot)
            await_sibling(other)
            add(other)

        flip = sibling - subj

        @pl.when(z + dist < n_z)
        def _():
            pair(subj + CORES * dist, subj + CORES * dist + flip)

        @pl.when(jnp.logical_and(z - dist >= 0, dist > 0))
        def _():
            pair(subj - CORES * dist, subj - CORES * dist + flip)

    n_tasks = n_perm * n_subj
    per_event = n_tasks // n_z
    acc[...] = jnp.zeros_like(acc)

    @pl.loop(0, n_z)
    def _(e):
        @pl.loop(0, per_event)
        def _(t):
            move(e * per_event + t)

        event(e, arrive)

    @pl.loop(n_z, n_events)
    def _(e):
        add_dist(e - n_z)
        event(e, arrive)

    @pl.loop(n_events - n_z, n_z)
    def _(dist):
        add_dist(dist)

    for p in range(n_perm):
        at = p * 2 * rows
        moved = acc[at + rows:at + 2 * rows]
        cross = jnp.sum(moved * (acc[at:at + rows] - kin_diag * moved), axis=0, keepdims=True)
        parts[p, 0:1] = cross

    def fin_copy(k, slot):
        other, device = partner(k)
        return pltpu.make_async_remote_copy(
            src_ref=parts.at[other // n_subj], dst_ref=final.at[slot],
            send_sem=fin_send.at[k], recv_sem=fin_recv.at[slot],
            device_id=device, device_id_type=MESH)

    @pl.loop(1, n_all)
    def _(k):
        fin_copy(k, me).start()

    final[me] = parts[perm]
    own_sends(lambda copy: copy.wait_send())

    @pl.loop(0, n_events)
    def _(e):
        event(e, drain)

    @pl.loop(1, n_all)
    def _(k):
        shuf_copy(k, me).wait_send()

    @pl.loop(1, n_all)
    def _(k):
        fin_copy(k, partner(k)[0]).wait_recv()

    count = n_subj * rows
    for q in range(n_perm):
        total = jnp.sum(final[q * n_subj:(q + 1) * n_subj], axis=0)
        scale = jnp.sqrt(jnp.float32(count)) * (total[1:2] / count + 1e-05)
        out_ref[:, q * cols:(q + 1) * cols] = total[0:1] / scale

    @pl.loop(1, n_all)
    def _(k):
        fin_copy(k, me).wait_send()


def per_device(n_perm, n_subj, kinship, phenotype, shuffle):
    rows, width = phenotype.shape
    cols = width // n_perm
    n_all = n_perm * n_subj
    DMA = pltpu.SemaphoreType.DMA
    out = pl.pallas_call(
        functools.partial(kernel, n_perm, n_subj),
        out_shape=jax.ShapeDtypeStruct((1, width), jnp.float32),
        in_specs=[pl.BlockSpec(memory_space=pltpu.VMEM)] * 3,
        out_specs=pl.BlockSpec(memory_space=pltpu.VMEM),
        scratch_shapes=[
            pltpu.VMEM((n_all, 1, rows), jnp.int32),
            pltpu.VMEM((n_perm, rows, rows), jnp.int32),
            pltpu.VMEM((n_subj, n_perm * 2 * rows, rows), jnp.bfloat16),
            pltpu.VMEM((n_subj, rows, cols), jnp.bfloat16),
            pltpu.VMEM((n_perm * 2 * rows, cols), jnp.float32),
            pltpu.VMEM((n_perm, 2, cols), jnp.float32),
            pltpu.VMEM((n_all, 2, cols), jnp.float32),
            DMA((n_all,)), DMA((n_all,)),
            DMA((3, HALVES)),
            DMA((n_subj, HALVES)), DMA((n_subj, HALVES)), DMA((n_subj, HALVES)),
            DMA((n_all,)), DMA((n_all,)),
        ],
        compiler_params=pltpu.CompilerParams(collective_id=0, has_side_effects=True),
    )(kinship, phenotype, shuffle.reshape(1, rows))
    return out.reshape(width)


def solution(mesh):
    in_specs = (P("subj", None), P("subj", "vert"), P(("perm", "subj")))
    out_specs = P(("perm", "vert"))
    body = functools.partial(per_device, mesh.shape["perm"], mesh.shape["subj"])
    return jax.shard_map(body, mesh=mesh, in_specs=in_specs, out_specs=out_specs, check_vma=False)
```

time: 86.4 us -> 36 us (0.42)
  Pallas kernels: 0 us -> 34.5 us
  blocking collectives: 28.8 us -> 0 us
  local copies, waits for them, and re-layouts: 20.5 us -> 1.28 us
  waiting for transfers between devices: 17.6 us -> 0 us
  between operations: 13.5 us -> 0.01 us
  matrix products: 5.08 us -> 0 us
    pallas_call x0 -> x1, Pallas kernels: none -> 34.5 us  [per_device(): pl.pallas_call(functools.partial(kernel, n_perm, n_subj), out_shape=jax.S...]
    all_gather x1 -> x0, waiting for transfers between devices: 16.9 us -> none  [per_device(): piece = lax.all_gather(phenotype, 'subj', axis=0, tiled=True)]
    psum x1 -> x0, blocking collectives: 15.1 us -> none  [per_device(): cross_all, squares_all = lax.psum((cross_term, squares), 'subj')]
    all_gather x1 -> x0, blocking collectives: 13.7 us -> none  [per_device(): shuffle_all = lax.all_gather(shuffle, 'subj', axis=0, tiled=True)]
    gather x2 -> x0, local copies, waits for them, and re-layouts: 9.99 us -> none  [the longest x1 7.5 us: per_device(): kin_moved = jnp.take(kinship, inverse, axis=1)]
    scatter x1 -> x0, local copies, waits for them, and re-layouts: 8.05 us -> none  [per_device(): inverse = jnp.zeros((subject_count,), jnp.int32).at[shuffle_all].set(jnp....]
    dot_general x2 -> x0, matrix products: 5.08 us -> none  [the longest x1 3.62 us: per_device(): picked = jnp.dot(picker, piece, preferred_element_type=jnp.float32)]
    dynamic_slice x1 -> x0, local copies, waits for them, and re-layouts: 0.92 us -> none  [per_device(): own_block = lax.dynamic_slice_in_dim(kinship, row_offset, row_count, 1)]
  transfers between devices with their start and end apart: 1 -> 0, of which waited for: 1 -> 0; matrix products, arithmetic and copies ran while one was open for 24% -> 0% of each run, Pallas kernels for 0% -> 0%
where the time goes in v1:
time: 36 us; the launch traced here: 35.8 us
  Pallas kernels  34.5 us (96%)
  local copies, waits for them, and re-layouts  1.28 us (4%)
    pallas_call x1, Pallas kernels, per_device(): pl.pallas_call(functools.partial(kernel, n_perm, n_subj), out_shape=jax.S...  34.5 us
    unnamed x1, local copies, waits for them, and re-layouts  1.28 us

profile of v1, /device:TPU:0, one launch (start us, length us, event | category | flops | bytes accessed | tf_op | source)
XLA Modules:
  0.0 35.8 jit_solution(10288389818502115558)
XLA Ops:
  0.0 34.5 %shard_map.37 = f32[1,1024]{1,0:T(1,128)} custom-call(bf16[256,2048]{1,0:T(8,128)(2,1)} %kin_ref.1, bf16[256,1024]{1,0:T(8,128)(2,1)} %phe_ref.1, s32[1,256]{1,0:T(1,128)} %bitcast.3), custom_call_target="tpu_custom_call" | custom-call | tf_op jit(solution)/shard_map/pallas_call | solution.py:240
  34.5 1.3 %copy.5 = f32[1024]{0:T(1024)} copy(f32[1024]{0:T(1024)} %bitcast.2) | data formatting | bytes 8192

commit v2 on v1

--- a/solution.py
+++ b/solution.py
@@ -9,13 +9,13 @@
 
 MESH = pl.DeviceIdType.MESH
 CORES = 2
-HALVES = 2
+HALVES = 4
 
 
 def kernel(
     n_perm, n_subj,
-    kin_ref, phe_ref, shf_ref, out_ref,
-    shuf, scol, moved_kin, gathered, acc, parts, final,
+    kin_hbm, phe_ref, shf_ref, out_ref,
+    kin_ref, load_sem, shuf, scol, moved_kin, gathered, acc, parts, final,
     shuf_send, shuf_recv, own_send, row_send, sib_send, row_recv, fin_send, fin_recv,
 ):
     perm, subj = lax.axis_index("perm"), lax.axis_index("subj")
@@ -34,6 +34,13 @@
         other = lax.rem(me + k, n_all)
         return other, {"perm": other // n_subj, "subj": lax.rem(other, n_subj)}
 
+    loads = (
+        pltpu.make_async_copy(
+            phe_ref.at[:, pl.ds(first_col, cols)], gathered.at[subj], load_sem.at[0]),
+        pltpu.make_async_copy(kin_hbm, kin_ref, load_sem.at[1]),
+    )
+    for load in loads:
+        load.start()
     barrier = pltpu.get_barrier_semaphore()
 
     @pl.loop(1, n_all)
@@ -82,9 +89,9 @@
 
     own_sends(lambda copy: copy.start())
     shuf[me] = shf_ref[...]
-    own = phe_ref[:, pl.ds(first_col, cols)]
-    gathered[subj] = own
-    own32 = own.astype(jnp.float32)
+    for load in loads:
+        load.wait()
+    own32 = gathered[subj].astype(jnp.float32)
     squares = jnp.sum(own32 * own32, axis=0, keepdims=True)
     for p in range(n_perm):
         parts[p, 1:2] = squares
@@ -169,10 +176,12 @@
             pair(subj - CORES * dist, subj - CORES * dist + flip)
 
     n_tasks = n_perm * n_subj
-    per_event = n_tasks // n_z
+    early = HALVES * n_z // 2
+    per_event = n_tasks // early
+    n_mixed = min(n_z - 1, n_events - early, early // (HALVES - 1) + 1)
     acc[...] = jnp.zeros_like(acc)
 
-    @pl.loop(0, n_z)
+    @pl.loop(0, early)
     def _(e):
         @pl.loop(0, per_event)
         def _(t):
@@ -180,12 +189,16 @@
 
         event(e, arrive)
 
-    @pl.loop(n_z, n_events)
-    def _(e):
-        add_dist(e - n_z)
+    @pl.loop(early, early + n_mixed)
+    def _(e):
+        add_dist(e - early)
         event(e, arrive)
 
-    @pl.loop(n_events - n_z, n_z)
+    @pl.loop(early + n_mixed, n_events)
+    def _(e):
+        event(e, arrive)
+
+    @pl.loop(n_mixed, n_z)
     def _(dist):
         add_dist(dist)
 
@@ -240,9 +253,11 @@
     out = pl.pallas_call(
         functools.partial(kernel, n_perm, n_subj),
         out_shape=jax.ShapeDtypeStruct((1, width), jnp.float32),
-        in_specs=[pl.BlockSpec(memory_space=pltpu.VMEM)] * 3,
+        in_specs=[pl.BlockSpec(memory_space=pl.ANY)] * 2 + [pl.BlockSpec(memory_space=pltpu.VMEM)],
         out_specs=pl.BlockSpec(memory_space=pltpu.VMEM),
         scratch_shapes=[
+            pltpu.VMEM(kinship.shape, jnp.bfloat16),
+            DMA((2,)),
             pltpu.VMEM((n_all, 1, rows), jnp.int32),
             pltpu.VMEM((n_perm, rows, rows), jnp.int32),
             pltpu.VMEM((n_subj, n_perm * 2 * rows, rows), jnp.bfloat16),

time: 36 us -> 34.5 us (0.958)
  Pallas kernels: 34.5 us -> 33.1 us
    pallas_call x1, Pallas kernels: 34.5 us -> 33.1 us  [per_device(): pl.pallas_call(functools.partial(kernel, n_perm, n_subj), out_shape=jax.S...]
where the time goes in v2:
time: 34.5 us; the launch traced here: 34.3 us
  Pallas kernels  33.1 us (96%)
  local copies, waits for them, and re-layouts  1.28 us (4%)
    pallas_call x1, Pallas kernels, per_device(): pl.pallas_call(functools.partial(kernel, n_perm, n_subj), out_shape=jax.S...  33.1 us
    unnamed x1, local copies, waits for them, and re-layouts  1.28 us

profile of v2, /device:TPU:0, one launch (start us, length us, event | category | flops | bytes accessed | tf_op | source)
XLA Modules:
  0.0 34.3 jit_solution(12380904538609347475)
XLA Ops:
  0.0 33.1 %shard_map.37 = f32[1,1024]{1,0:T(1,128)} custom-call(bf16[256,2048]{1,0:T(8,128)(2,1)} %kin_hbm.1, bf16[256,1024]{1,0:T(8,128)(2,1)} %phe_ref.1, s32[1,256]{1,0:T(1,128)} %bitcast.3), custom_call_target="tpu_custom_call" | custom-call | tf_op jit(solution)/shard_map/pallas_call | solution.py:253
  33.1 1.3 %copy.5 = f32[1024]{0:T(1024)} copy(f32[1024]{0:T(1024)} %bitcast.2) | data formatting | bytes 8192

commit v3 on v2

--- a/solution.py
+++ b/solution.py
@@ -10,12 +10,13 @@
 MESH = pl.DeviceIdType.MESH
 CORES = 2
 HALVES = 4
+BEFORE = 2
 
 
 def kernel(
     n_perm, n_subj,
     kin_hbm, phe_ref, shf_ref, out_ref,
-    kin_ref, load_sem, shuf, scol, moved_kin, gathered, acc, parts, final,
+    kin_ref, load_sem, waves, shuf, scol, moved_kin, gathered, acc, parts, final,
     shuf_send, shuf_recv, own_send, row_send, sib_send, row_recv, fin_send, fin_recv,
 ):
     perm, subj = lax.axis_index("perm"), lax.axis_index("subj")
@@ -43,11 +44,61 @@
         load.start()
     barrier = pltpu.get_barrier_semaphore()
 
-    @pl.loop(1, n_all)
-    def _(k):
-        pl.semaphore_signal(barrier, inc=1, device_id=partner(k)[1], device_id_type=MESH)
-
-    pl.semaphore_wait(barrier, n_all - 1)
+    has_left, has_right = z > 0, z < n_z - 1
+
+    def signal(sem, **device):
+        pl.semaphore_signal(sem, inc=1, device_id=device, device_id_type=MESH)
+
+    def signal_perms(sem):
+        for k in range(1, n_perm):
+            signal(sem, perm=lax.rem(perm + k, n_perm))
+
+    @pl.when(has_left)
+    def _():
+        signal(barrier, subj=subj - CORES)
+
+    @pl.when(has_right)
+    def _():
+        signal(barrier, subj=subj + CORES)
+
+    signal(barrier, subj=sibling)
+    signal_perms(barrier)
+    pl.semaphore_wait(
+        barrier, n_perm + has_left.astype(jnp.int32) + has_right.astype(jnp.int32))
+
+    def wave_right():
+        @pl.when(has_left)
+        def _():
+            pl.semaphore_wait(waves.at[0], 1)
+
+        @pl.when(has_right)
+        def _():
+            signal(waves.at[0], subj=subj + CORES)
+
+    def wave_left():
+        @pl.when(has_right)
+        def _():
+            pl.semaphore_wait(waves.at[1], 1)
+
+        @pl.when(has_left)
+        def _():
+            signal(waves.at[1], subj=subj - CORES)
+
+    def all_ready():
+        @pl.when(z < n_z // 2)
+        def _():
+            wave_right()
+            wave_left()
+
+        @pl.when(z >= n_z // 2)
+        def _():
+            wave_left()
+            wave_right()
+
+        signal(waves.at[2], subj=sibling)
+        pl.semaphore_wait(waves.at[2], 1)
+        signal_perms(waves.at[3])
+        pl.semaphore_wait(waves.at[3], n_perm - 1)
 
     def half(h):
         return pl.ds(pl.multiple_of(h * piece, piece), piece)
@@ -71,12 +122,8 @@
             send_sem=shuf_send.at[k], recv_sem=shuf_recv.at[slot],
             device_id=partner(k)[1], device_id_type=MESH)
 
-    @pl.loop(1, n_all)
-    def _(k):
-        shuf_copy(k, me).start()
-
-    def own_sends(act):
-        for h in range(HALVES):
+    def own_sends(first, last, act):
+        for h in range(first, last):
             @pl.when(z > 0)
             def _():
                 act(own_copy(h, 0, subj - CORES))
@@ -87,7 +134,14 @@
 
             act(own_copy(h, 2, sibling))
 
-    own_sends(lambda copy: copy.start())
+    own_sends(0, HALVES - 1, lambda copy: copy.start())
+    all_ready()
+
+    @pl.loop(1, n_all)
+    def _(k):
+        shuf_copy(k, me).start()
+
+    own_sends(HALVES - 1, HALVES, lambda copy: copy.start())
     shuf[me] = shf_ref[...]
     for load in loads:
         load.wait()
@@ -102,14 +156,6 @@
         jnp.where(down == across, kin_ref[:, own_cols].astype(jnp.float32), 0.0),
         axis=1, keepdims=True)
 
-    @pl.loop(1, n_all)
-    def _(k):
-        shuf_copy(k, partner(k)[0]).wait_recv()
-
-    for p in range(n_perm):
-        mine = shuf[p * n_subj + subj]
-        scol[p] = jnp.transpose(jnp.broadcast_to(mine, (rows, rows)))
-
     def move(task):
         p, block = task // n_subj, lax.rem(task, n_subj)
         base = down + block * rows
@@ -176,16 +222,29 @@
             pair(subj - CORES * dist, subj - CORES * dist + flip)
 
     n_tasks = n_perm * n_subj
-    early = HALVES * n_z // 2
-    per_event = n_tasks // early
+    busy = HALVES * n_z // 2
+    per_event = n_tasks // busy
+    early = min(BEFORE + busy, n_events)
     n_mixed = min(n_z - 1, n_events - early, early // (HALVES - 1) + 1)
     acc[...] = jnp.zeros_like(acc)
-
-    @pl.loop(0, early)
-    def _(e):
+    for e in range(BEFORE):
+        event(e, arrive)
+
+    @pl.loop(1, n_all)
+    def _(k):
+        shuf_copy(k, partner(k)[0]).wait_recv()
+
+    for p in range(n_perm):
+        mine = shuf[p * n_subj + subj]
+        scol[p] = jnp.transpose(jnp.broadcast_to(mine, (rows, rows)))
+
+    @pl.loop(0, busy)
+    def _(turn):
         @pl.loop(0, per_event)
         def _(t):
-            move(e * per_event + t)
+            move(turn * per_event + t)
+
+        e = BEFORE + turn
 
         event(e, arrive)
 
@@ -220,7 +279,7 @@
         fin_copy(k, me).start()
 
     final[me] = parts[perm]
-    own_sends(lambda copy: copy.wait_send())
+    own_sends(0, HALVES, lambda copy: copy.wait_send())
 
     @pl.loop(0, n_events)
     def _(e):
@@ -258,6 +317,7 @@
         scratch_shapes=[
             pltpu.VMEM(kinship.shape, jnp.bfloat16),
             DMA((2,)),
+            pltpu.SemaphoreType.REGULAR((4,)),
             pltpu.VMEM((n_all, 1, rows), jnp.int32),
             pltpu.VMEM((n_perm, rows, rows), jnp.int32),
             pltpu.VMEM((n_subj, n_perm * 2 * rows, rows), jnp.bfloat16),

time: 34.5 us -> 34.1 us (0.988)
  Pallas kernels: 33.1 us -> 32.6 us
    pallas_call x1, Pallas kernels: 33.1 us -> 32.6 us  [per_device(): pl.pallas_call(functools.partial(kernel, n_perm, n_subj), out_shape=jax.S...]
where the time goes in v3:
time: 34.1 us; the launch traced here: 33.9 us
  Pallas kernels  32.6 us (96%)
  local copies, waits for them, and re-layouts  1.28 us (4%)
    pallas_call x1, Pallas kernels, per_device(): pl.pallas_call(functools.partial(kernel, n_perm, n_subj), out_shape=jax.S...  32.6 us
    unnamed x1, local copies, waits for them, and re-layouts  1.28 us

profile of v3, /device:TPU:0, one launch (start us, length us, event | category | flops | bytes accessed | tf_op | source)
XLA Modules:
  0.0 33.9 jit_solution(17781907993882991159)
XLA Ops:
  0.0 32.6 %shard_map.37 = f32[1,1024]{1,0:T(1,128)} custom-call(bf16[256,2048]{1,0:T(8,128)(2,1)} %kin_hbm.1, bf16[256,1024]{1,0:T(8,128)(2,1)} %phe_ref.1, s32[1,256]{1,0:T(1,128)} %bitcast.3), custom_call_target="tpu_custom_call" | custom-call | tf_op jit(solution)/shard_map/pallas_call | solution.py:312
  32.6 1.3 %copy.5 = f32[1024]{0:T(1024)} copy(f32[1024]{0:T(1024)} %bitcast.2) | data formatting | bytes 8192

commit v4 on v3

--- a/solution.py
+++ b/solution.py
@@ -9,14 +9,14 @@
 
 MESH = pl.DeviceIdType.MESH
 CORES = 2
-HALVES = 4
-BEFORE = 2
+HALVES = 8
+BEFORE = 4
 
 
 def kernel(
     n_perm, n_subj,
     kin_hbm, phe_ref, shf_ref, out_ref,
-    kin_ref, load_sem, waves, shuf, scol, moved_kin, gathered, acc, parts, final,
+    kin_ref, load_sem, waves, sq_own, sq_all, sq_send, sq_recv, shuf, scol, moved_kin, gathered, acc, parts, final,
     shuf_send, shuf_recv, own_send, row_send, sib_send, row_recv, fin_send, fin_recv,
 ):
     perm, subj = lax.axis_index("perm"), lax.axis_index("subj")
@@ -147,8 +147,19 @@
         load.wait()
     own32 = gathered[subj].astype(jnp.float32)
     squares = jnp.sum(own32 * own32, axis=0, keepdims=True)
-    for p in range(n_perm):
-        parts[p, 1:2] = squares
+    sq_own[...] = squares
+    sq_all[me] = squares
+
+    def sq_copy(k, slot):
+        return pltpu.make_async_remote_copy(
+            src_ref=sq_own, dst_ref=sq_all.at[slot],
+            send_sem=sq_send.at[k], recv_sem=sq_recv.at[slot],
+            device_id=partner(k)[1], device_id_type=MESH)
+
+    @pl.loop(1, n_all)
+    def _(k):
+        sq_copy(k, me).start()
+
     own_cols = pl.ds(pl.multiple_of(subj * rows, rows), rows)
     down = lax.broadcasted_iota(jnp.int32, (rows, rows), 0)
     across = lax.broadcasted_iota(jnp.int32, (rows, rows), 1)
@@ -225,7 +236,6 @@
     busy = HALVES * n_z // 2
     per_event = n_tasks // busy
     early = min(BEFORE + busy, n_events)
-    n_mixed = min(n_z - 1, n_events - early, early // (HALVES - 1) + 1)
     acc[...] = jnp.zeros_like(acc)
     for e in range(BEFORE):
         event(e, arrive)
@@ -248,24 +258,23 @@
 
         event(e, arrive)
 
-    @pl.loop(early, early + n_mixed)
-    def _(e):
-        add_dist(e - early)
-        event(e, arrive)
-
-    @pl.loop(early + n_mixed, n_events)
-    def _(e):
-        event(e, arrive)
-
-    @pl.loop(n_mixed, n_z)
-    def _(dist):
-        add_dist(dist)
+    late = n_events - early
+
+    @pl.loop(0, late)
+    def _(turn):
+        @pl.loop(turn * (n_z - 1) // late, (turn + 1) * (n_z - 1) // late)
+        def _(dist):
+            add_dist(dist)
+
+        event(early + turn, arrive)
+
+    add_dist(n_z - 1)
 
     for p in range(n_perm):
         at = p * 2 * rows
         moved = acc[at + rows:at + 2 * rows]
         cross = jnp.sum(moved * (acc[at:at + rows] - kin_diag * moved), axis=0, keepdims=True)
-        parts[p, 0:1] = cross
+        parts[p] = cross
 
     def fin_copy(k, slot):
         other, device = partner(k)
@@ -288,16 +297,22 @@
     @pl.loop(1, n_all)
     def _(k):
         shuf_copy(k, me).wait_send()
+        sq_copy(k, me).wait_send()
+        sq_copy(k, partner(k)[0]).wait_recv()
+
+    count = n_subj * rows
+    scales = [
+        jnp.sqrt(jnp.float32(count))
+        * (jnp.sum(sq_all[q * n_subj:(q + 1) * n_subj], axis=0) / count + 1e-05)
+        for q in range(n_perm)]
 
     @pl.loop(1, n_all)
     def _(k):
         fin_copy(k, partner(k)[0]).wait_recv()
 
-    count = n_subj * rows
     for q in range(n_perm):
         total = jnp.sum(final[q * n_subj:(q + 1) * n_subj], axis=0)
-        scale = jnp.sqrt(jnp.float32(count)) * (total[1:2] / count + 1e-05)
-        out_ref[:, q * cols:(q + 1) * cols] = total[0:1] / scale
+        out_ref[:, q * cols:(q + 1) * cols] = total / scales[q]
 
     @pl.loop(1, n_all)
     def _(k):
@@ -318,13 +333,16 @@
             pltpu.VMEM(kinship.shape, jnp.bfloat16),
             DMA((2,)),
             pltpu.SemaphoreType.REGULAR((4,)),
+            pltpu.VMEM((1, cols), jnp.float32),
+            pltpu.VMEM((n_all, 1, cols), jnp.float32),
+            DMA((n_all,)), DMA((n_all,)),
             pltpu.VMEM((n_all, 1, rows), jnp.int32),
             pltpu.VMEM((n_perm, rows, rows), jnp.int32),
             pltpu.VMEM((n_subj, n_perm * 2 * rows, rows), jnp.bfloat16),
             pltpu.VMEM((n_subj, rows, cols), jnp.bfloat16),
             pltpu.VMEM((n_perm * 2 * rows, cols), jnp.float32),
-            pltpu.VMEM((n_perm, 2, cols), jnp.float32),
-            pltpu.VMEM((n_all, 2, cols), jnp.float32),
+            pltpu.VMEM((n_perm, 1, cols), jnp.float32),
+            pltpu.VMEM((n_all, 1, cols), jnp.float32),
             DMA((n_all,)), DMA((n_all,)),
             DMA((3, HALVES)),
             DMA((n_subj, HALVES)), DMA((n_subj, HALVES)), DMA((n_subj, HALVES)),

time: 34.1 us -> 35.6 us (1.044)
  Pallas kernels: 32.6 us -> 34.2 us
    pallas_call x1, Pallas kernels: 32.6 us -> 34.2 us  [per_device(): pl.pallas_call(functools.partial(kernel, n_perm, n_subj), out_shape=jax.S...]
where the time goes in v4:
time: 35.6 us; the launch traced here: 35.4 us
  Pallas kernels  34.2 us (96%)
  local copies, waits for them, and re-layouts  1.28 us (4%)
    pallas_call x1, Pallas kernels, per_device(): pl.pallas_call(functools.partial(kernel, n_perm, n_subj), out_shape=jax.S...  34.2 us
    unnamed x1, local copies, waits for them, and re-layouts  1.28 us

profile of v4, /device:TPU:0, one launch (start us, length us, event | category | flops | bytes accessed | tf_op | source)
XLA Modules:
  0.0 35.4 jit_solution(1259034884034735489)
XLA Ops:
  0.0 34.2 %shard_map.37 = f32[1,1024]{1,0:T(1,128)} custom-call(bf16[256,2048]{1,0:T(8,128)(2,1)} %kin_hbm.1, bf16[256,1024]{1,0:T(8,128)(2,1)} %phe_ref.1, s32[1,256]{1,0:T(1,128)} %bitcast.3), custom_call_target="tpu_custom_call" | custom-call | tf_op jit(solution)/shard_map/pallas_call | solution.py:327
  34.2 1.3 %copy.5 = f32[1024]{0:T(1024)} copy(f32[1024]{0:T(1024)} %bitcast.2) | data formatting | bytes 8192

commit v5 on v3

--- a/solution.py
+++ b/solution.py
@@ -225,7 +225,6 @@
     busy = HALVES * n_z // 2
     per_event = n_tasks // busy
     early = min(BEFORE + busy, n_events)
-    n_mixed = min(n_z - 1, n_events - early, early // (HALVES - 1) + 1)
     acc[...] = jnp.zeros_like(acc)
     for e in range(BEFORE):
         event(e, arrive)
@@ -248,18 +247,17 @@
 
         event(e, arrive)
 
-    @pl.loop(early, early + n_mixed)
-    def _(e):
-        add_dist(e - early)
-        event(e, arrive)
-
-    @pl.loop(early + n_mixed, n_events)
-    def _(e):
-        event(e, arrive)
-
-    @pl.loop(n_mixed, n_z)
-    def _(dist):
-        add_dist(dist)
+    late = n_events - early
+
+    @pl.loop(0, late)
+    def _(turn):
+        @pl.loop(turn * (n_z - 1) // late, (turn + 1) * (n_z - 1) // late)
+        def _(dist):
+            add_dist(dist)
+
+        event(early + turn, arrive)
+
+    add_dist(n_z - 1)
 
     for p in range(n_perm):
         at = p * 2 * rows
@@ -267,16 +265,23 @@
         cross = jnp.sum(moved * (acc[at:at + rows] - kin_diag * moved), axis=0, keepdims=True)
         parts[p, 0:1] = cross
 
+    per_z = n_all // n_z
+    far_low = (z >= n_z // 2).astype(jnp.int32)
+
     def fin_copy(k, slot):
-        other, device = partner(k)
-        return pltpu.make_async_remote_copy(
-            src_ref=parts.at[other // n_subj], dst_ref=final.at[slot],
+        turn, rest = k // per_z, lax.rem(k, per_z)
+        to_z = far_low * turn + (1 - far_low) * (n_z - 1 - turn)
+        to_perm, to_subj = rest // CORES, to_z * CORES + lax.rem(rest, CORES)
+        copy = pltpu.make_async_remote_copy(
+            src_ref=parts.at[to_perm], dst_ref=final.at[slot],
             send_sem=fin_send.at[k], recv_sem=fin_recv.at[slot],
-            device_id=device, device_id_type=MESH)
-
-    @pl.loop(1, n_all)
-    def _(k):
-        fin_copy(k, me).start()
+            device_id={"perm": to_perm, "subj": to_subj}, device_id_type=MESH)
+        return copy, to_perm * n_subj + to_subj != me
+
+    @pl.loop(0, n_all)
+    def _(k):
+        copy, other = fin_copy(k, me)
+        pl.when(other)(copy.start)
 
     final[me] = parts[perm]
     own_sends(0, HALVES, lambda copy: copy.wait_send())
@@ -291,7 +296,7 @@
 
     @pl.loop(1, n_all)
     def _(k):
-        fin_copy(k, partner(k)[0]).wait_recv()
+        fin_copy(0, partner(k)[0])[0].wait_recv()
 
     count = n_subj * rows
     for q in range(n_perm):
@@ -299,9 +304,10 @@
         scale = jnp.sqrt(jnp.float32(count)) * (total[1:2] / count + 1e-05)
         out_ref[:, q * cols:(q + 1) * cols] = total[0:1] / scale
 
-    @pl.loop(1, n_all)
-    def _(k):
-        fin_copy(k, me).wait_send()
+    @pl.loop(0, n_all)
+    def _(k):
+        copy, other = fin_copy(k, me)
+        pl.when(other)(copy.wait_send)
 
 
 def per_device(n_perm, n_subj, kinship, phenotype, shuffle):

time: 34.1 us -> 34 us (level)
  no operation moved by 1% of the time
where the time goes in v5:
time: 34 us; the launch traced here: 33.8 us
  Pallas kernels  32.5 us (96%)
  local copies, waits for them, and re-layouts  1.28 us (4%)
    pallas_call x1, Pallas kernels, per_device(): pl.pallas_call(functools.partial(kernel, n_perm, n_subj), out_shape=jax.S...  32.5 us
    unnamed x1, local copies, waits for them, and re-layouts  1.28 us

profile of v5, /device:TPU:0, one launch (start us, length us, event | category | flops | bytes accessed | tf_op | source)
XLA Modules:
  0.0 33.8 jit_solution(391036056867472700)
XLA Ops:
  0.0 32.5 %shard_map.37 = f32[1,1024]{1,0:T(1,128)} custom-call(bf16[256,2048]{1,0:T(8,128)(2,1)} %kin_hbm.1, bf16[256,1024]{1,0:T(8,128)(2,1)} %phe_ref.1, s32[1,256]{1,0:T(1,128)} %bitcast.3), custom_call_target="tpu_custom_call" | custom-call | tf_op jit(solution)/shard_map/pallas_call | solution.py:318
  32.5 1.3 %copy.5 = f32[1024]{0:T(1024)} copy(f32[1024]{0:T(1024)} %bitcast.2) | data formatting | bytes 8192

commit v6 on v5

--- a/solution.py
+++ b/solution.py
@@ -298,11 +298,9 @@
     def _(k):
         fin_copy(0, partner(k)[0])[0].wait_recv()
 
-    count = n_subj * rows
     for q in range(n_perm):
         total = jnp.sum(final[q * n_subj:(q + 1) * n_subj], axis=0)
-        scale = jnp.sqrt(jnp.float32(count)) * (total[1:2] / count + 1e-05)
-        out_ref[:, q * cols:(q + 1) * cols] = total[0:1] / scale
+        out_ref[:, q * cols:(q + 1) * cols] = total
 
     @pl.loop(0, n_all)
     def _(k):
@@ -317,7 +315,7 @@
     DMA = pltpu.SemaphoreType.DMA
     out = pl.pallas_call(
         functools.partial(kernel, n_perm, n_subj),
-        out_shape=jax.ShapeDtypeStruct((1, width), jnp.float32),
+        out_shape=jax.ShapeDtypeStruct((2, width), jnp.float32),
         in_specs=[pl.BlockSpec(memory_space=pl.ANY)] * 2 + [pl.BlockSpec(memory_space=pltpu.VMEM)],
         out_specs=pl.BlockSpec(memory_space=pltpu.VMEM),
         scratch_shapes=[
@@ -338,7 +336,8 @@
         ],
         compiler_params=pltpu.CompilerParams(collective_id=0, has_side_effects=True),
     )(kinship, phenotype, shuffle.reshape(1, rows))
-    return out.reshape(width)
+    count = n_subj * rows
+    return out[0] / (jnp.sqrt(jnp.float32(count)) * (out[1] / count + 1e-05))
 
 
 def solution(mesh):

time: 34 us -> 34.1 us (level)
  other arithmetic: 0 us -> 1.38 us
  local copies, waits for them, and re-layouts: 1.28 us -> 0 us
    div x0 -> x1, other arithmetic: none -> 1.38 us  [per_device(): return out[0] / (jnp.sqrt(jnp.float32(count)) * (out[1] / count + 1e-05))]
    unnamed x1 -> x0, local copies, waits for them, and re-layouts: 1.28 us -> none
where the time goes in v6:
time: 34.1 us; the launch traced here: 33.9 us
  Pallas kernels  32.5 us (95%)
  other arithmetic  1.38 us (4%)
    pallas_call x1, Pallas kernels, per_device(): pl.pallas_call(functools.partial(kernel, n_perm, n_subj), out_shape=jax.S...  32.5 us
    div x1, other arithmetic, per_device(): return out[0] / (jnp.sqrt(jnp.float32(count)) * (out[1] / count + 1e-05))  1.38 us

profile of v6, /device:TPU:0, one launch (start us, length us, event | category | flops | bytes accessed | tf_op | source)
XLA Modules:
  0.0 33.9 jit_solution(467899814714624337)
XLA Ops:
  0.0 32.5 %shard_map.37 = f32[2,1024]{1,0:T(2,128)} custom-call(bf16[256,2048]{1,0:T(8,128)(2,1)} %kin_hbm.1, bf16[256,1024]{1,0:T(8,128)(2,1)} %phe_ref.1, s32[1,256]{1,0:T(1,128)} %bitcast.2), custom_call_target="tpu_custom_call" | custom-call | tf_op jit(solution)/shard_map/pallas_call | solution.py:316
  32.5 1.4 %multiply_divide_fusion = f32[1,1024]{1,0:T(1,128)} fusion(f32[2,1024]{1,0:T(2,128)} %shard_map.37), kind=kLoop, calls=%fused_computation | loop fusion | flops 4096 | bytes 12288 | tf_op jit(solution)/shard_map/div | solution.py:340
